TPU v7x, 32 devices: a whole 2x2x4 slice. The times are simulated.
32 devices in a mesh: tile: 8 (over y, x, core), grp: 4 (over z).
Axes of the slice: x: 2, y: 2, z: 4, core: 2. Of those that a mesh axis runs over, the one named last changes fastest.
Arguments:
- amplitudes: bfloat16 [2, 64, 4096], P(None, 'tile', 'grp'), may hold values from -6 to 6
- integrals: bfloat16 [8, 16, 256, 256], P('tile', 'grp'), may hold values from -0.1875 to 0.1875
- slot_cd: int32 [8, 16], P('tile'), may hold values from 0 to 3
- slot_ab: int32 [8, 16], P('tile'), may hold values from 0 to 2, as said below
Outputs:
- ladder: bfloat16 [2, 64, 4096], P(None, 'grp', 'tile')
Inputs may be any that keep to these rules, and one draw needn't show every extreme that they name: `slot_ab`: 2 marks an empty slot. In every grid column one index of grp has all of its 4 slots live.
All inputs are finite; a program needn't handle non-finite values.
Results may differ from a plain program's by a relative error of at most 0.0085.
Values may be sent and summed in bfloat16 or wider, within the bound.
A program may use at most 64 MiB of HBM per device.

v0:
```python
import jax
import jax.numpy as jnp
from jax import lax
from jax.sharding import PartitionSpec as P

NT_DEV = 2
BATCH = 2


def accumulate(slot_operands, slot_tiles, ab_list):
    row_count = slot_operands.shape[0]
    widths = slot_tiles.shape[-1]
    products = jnp.einsum(
        "rsc,scd->rsd", slot_operands, slot_tiles, preferred_element_type=jnp.float32
    )
    select = (ab_list[:, None] == jnp.arange(NT_DEV, dtype=jnp.int32)[None, :]).astype(jnp.float32)
    summed = jnp.einsum("rsd,sa->rad", products, select)
    return summed.reshape(row_count, NT_DEV * widths)


def per_device(amplitudes, integrals, slot_cd, slot_ab):
    groups = lax.axis_size("grp")
    own_index = lax.axis_index("grp")
    widths = integrals.shape[-1]
    pairs = amplitudes.shape[1] * lax.axis_size("tile")
    cd_table = slot_cd[0].reshape(groups, groups)
    ab_table = slot_ab[0].reshape(groups, groups)
    own_tiles = integrals[0]
    moved_tiles = lax.all_to_all(own_tiles, "grp", split_axis=0, concat_axis=0, tiled=True)
    cd_list = lax.dynamic_index_in_dim(cd_table, own_index, 1, keepdims=False)
    ab_list = lax.dynamic_index_in_dim(ab_table, own_index, 1, keepdims=False)
    outputs = []
    for batch_index in range(BATCH):
        slab_block = lax.all_gather(amplitudes[batch_index], "tile", axis=0, tiled=True)
        blocks = slab_block.reshape(pairs, slab_block.shape[1] // widths, widths)
        operands = jnp.take(blocks, cd_list, axis=1)
        full_terms = accumulate(operands, moved_tiles, ab_list)
        partial_value = lax.psum_scatter(full_terms, "grp", scatter_dimension=0, tiled=True)
        outputs.append((0.5 * partial_value).astype(jnp.bfloat16))
    return jnp.stack(outputs)


def solution(mesh):
    return jax.shard_map(
        per_device,
        mesh=mesh,
        in_specs=(
            P(None, "tile", "grp"),
            P("tile", "grp", None, None),
            P("tile", None),
            P("tile", None),
        ),
        out_specs=P(None, "grp", "tile"),
        check_vma=False,
    )
```

profile of v0, /device:TPU:0, one launch (start us, length us, event | category | flops | bytes accessed | tf_op | source)
XLA Modules:
  0.0 84.7 jit_solution(4557133586597225766)
XLA Ops:
  6.5 6.5 %all-to-all-start = ((bf16[4,256,256]{2,1,0:T(8,128)(2,1)}), bf16[4,256,256]{2,1,0:T(8,128)(2,1)S(1)}, u32[]{:S(2)}, u32[]{:S(2)}) async-start(bf16[4,256,256]{2,1,0:T(8,128)(2,1)} %bitcast.28), calls=%async_computation | async-start | bytes 1048576 | tf_op jit(solution)/shard_map/all_to_all | solution.py:29
  13.0 0.5 broadcast.76
  13.5 0.1 copy-done.1
  13.7 0.7 reduce.10
  14.4 0.7 reduce.11
  15.0 0.1 reshape_squeeze.6
  15.1 0.1 reshape_squeeze.7
  15.2 0.2 dynamic-slice_reduce_fusion.1
  15.4 0.2 dynamic-slice_reduce_fusion
  15.6 9.2 %all-gather = bf16[1,64,1024]{2,1,0:T(8,128)(2,1)S(1)} all-gather(bf16[1,8,1024]{2,1,0:T(8,128)(2,1)S(1)} %get-tuple-element.6), channel_id=2, replica_groups=mesh['tile'=8,'grp'=4] {'tile'}, dimensions={1}, use_global_device_ids=true | all-gather | bytes 147456 | tf_op jit(solution)/shard_map/all_gather | solution.py:34
  24.9 9.2 %all-gather.1 = bf16[1,64,1024]{2,1,0:T(8,128)(2,1)S(1)} all-gather(bf16[1,8,1024]{2,1,0:T(8,128)(2,1)S(1)} %get-tuple-element.7), channel_id=3, replica_groups=mesh['tile'=8,'grp'=4] {'tile'}, dimensions={1}, use_global_device_ids=true | all-gather | bytes 147456 | tf_op jit(solution)/shard_map/all_gather | solution.py:34
  34.2 0.6 gather_fusion
  34.8 0.6 gather_fusion.1
  35.4 0.2 convolution_bitcast_fusion.1
  35.6 0.2 fusion.2
  35.8 0.7 copy.9
  36.6 0.2 convolution_bitcast_fusion
  36.8 0.2 fusion
  37.1 0.7 copy.10
  37.7 18.9 %reduce-scatter.3.cloned.1.call-done = f32[16,512]{1,0:T(8,128)} async-done(((f32[64,512]{1,0:T(8,128)}), f32[16,512]{1,0:T(8,128)}) %reduce-scatter.3.cloned.1.call-update) | async-done | bytes 32784 | tf_op jit(solution)/shard_map/reduce_scatter | solution.py:38
  56.6 0.8 fusion.12
  57.4 19.1 %reduce-scatter.5.cloned.1.call-done = f32[16,512]{1,0:T(8,128)} async-done(((f32[64,512]{1,0:T(8,128)}), f32[16,512]{1,0:T(8,128)}) %reduce-scatter.5.cloned.1.call-update) | async-done | bytes 32784 | tf_op jit(solution)/shard_map/reduce_scatter | solution.py:38
  76.5 0.8 fusion.13
  77.3 0.6 pad_maximum_fusion
  (18 shorter events, 0.3 us)
Async XLA Ops:
  6.5 9.0 %copy-start = (bf16[2,8,1024]{2,1,0:T(8,128)(2,1)S(1)}, bf16[2,8,1024]{2,1,0:T(8,128)(2,1)}, u32[]{:S(2)}) copy-start(bf16[2,8,1024]{2,1,0:T(8,128)(2,1)} %param.6) | copy-start | bytes 98308
  6.5 28.8 %all-to-all-start = ((bf16[4,256,256]{2,1,0:T(8,128)(2,1)}), bf16[4,256,256]{2,1,0:T(8,128)(2,1)S(1)}, u32[]{:S(2)}, u32[]{:S(2)}) async-start(bf16[4,256,256]{2,1,0:T(8,128)(2,1)} %bitcast.28), calls=%async_computation | async-start | bytes 1048576 | tf_op jit(solution)/shard_map/all_to_all | solution.py:29
  13.0 43.6 %reduce-scatter.3.cloned.1.call-start = ((), (), s32[]{:S(2)}) async-start(), calls=%async_computation.3 | async-start | bytes 163840 | tf_op jit(solution)/shard_map/reduce_scatter | solution.py:38
  13.0 0.7 copy-start.1
  13.7 0.7 copy-start.2
  36.5 40.0 %reduce-scatter.5.cloned.1.call-start = ((), (), s32[]{:S(2)}) async-start(), calls=%async_computation.4 | async-start | bytes 163840 | tf_op jit(solution)/shard_map/reduce_scatter | solution.py:38
Sparse Core Ops, SparseCore 0:
  36.7 19.9 reduce-scatter.2
  58.9 17.6 reduce-scatter.4
where the time goes:
time: 85.2 us; the launch traced here: 84.7 us
  waiting for transfers between devices  38.1 us (45%)
  blocking collectives  18.4 us (22%)
  between operations  13.5 us (16%)
  starting transfers between devices  6.52 us (8%)
  local copies, waits for them, and re-layouts  3.82 us (4%)
  other arithmetic  3.5 us (4%)
  matrix products  0.92 us (1%)
    reduce_scatter x2, waiting for transfers between devices, per_device(): lax.psum_scatter(full_terms, 'grp', scatter_dimension=0, tiled=True)  38 us
    all_gather x2, blocking collectives, per_device(): lax.all_gather(amplitudes[batch_index], 'tile', axis=0, tiled=True)  18.4 us
    all_to_all x1, starting transfers between devices, per_device(): lax.all_to_all(own_tiles, 'grp', split_axis=0, concat_axis=0, tiled=True)  6.48 us
    another operation x3, other arithmetic, per_device(): return jnp.stack(outputs)  2.14 us
    unnamed x9, local copies, waits for them, and re-layouts  1.99 us
  transfers between devices with their start and end apart: 3, of which 2 were waited for; matrix products, arithmetic and copies ran while one was open for 7% of the time, Pallas kernels for 0%

commit v1 on v0

--- a/solution.py
+++ b/solution.py
@@ -1,10 +1,194 @@
+import functools
+
 import jax
 import jax.numpy as jnp
 from jax import lax
+from jax.experimental import pallas as pl
+from jax.experimental.pallas import tpu as pltpu
 from jax.sharding import PartitionSpec as P
 
+MESH = pl.DeviceIdType.MESH
 NT_DEV = 2
 BATCH = 2
+GATHER_LIMIT = 8 * 2**20
+ORDERS = (("z", 1, 2, 0), (2, 1, "z", 0))
+HOP = {"z": 2.6, 0: 1.1}
+
+
+def flip(index, mask):
+    bit = 1
+    while bit <= mask:
+        if mask & bit:
+            index = index + bit * (1 - 2 * lax.rem(lax.div(index, jnp.int32(bit)), jnp.int32(2)))
+        bit *= 2
+    return index
+
+
+def schedule(groups, tiles):
+    bits = tiles.bit_length() - 1
+    events, sends = [], {}
+    for half in range(BATCH):
+        named = ORDERS[half % len(ORDERS)]
+        extra = [b for b in range(bits) if b not in named]
+        order = [d for d in named if d == "z" or d < bits]
+        order = order[:-1] + extra + order[-1:]
+        frontier = [((half, 0, 0), -1, 0.0)]
+        while frontier:
+            node, place, when = frontier.pop(0)
+            sends[node] = []
+            for at in range(place + 1, len(order)):
+                dim = order[at]
+                if dim == "z":
+                    reached = [(half, dz, node[2]) for dz in range(1, groups)]
+                else:
+                    reached = [(half, node[1], node[2] | (1 << dim))]
+                for child in reached:
+                    arrives = when + HOP.get(dim, 2.0)
+                    sends[node].append((child, dim))
+                    events.append((arrives, child))
+                    frontier.append((child, at, arrives))
+    events.sort()
+    return [child for _, child in events], sends
+
+
+def kernel(groups, tiles, amp_ref, int_ref, cd_ref, ab_ref, out_ref, buf, tile_buf, acc, send_buf, sums_buf,
+           cd_smem, ab_smem, local_sem, send_sem, recv_sem, rs_send, rs_recv):
+    g, t = lax.axis_index("grp"), lax.axis_index("tile")
+    widths = int_ref.shape[-1]
+    rows = out_ref.shape[1]
+    bits = tiles.bit_length() - 1
+
+    locals_ = [pltpu.make_async_copy(amp_ref.at[h], buf.at[h, g, t], local_sem.at[h]) for h in range(BATCH)]
+    cd_copy = pltpu.make_async_copy(cd_ref, cd_smem, local_sem.at[BATCH])
+    ab_copy = pltpu.make_async_copy(ab_ref, ab_smem, local_sem.at[BATCH + 1])
+    int_copy = pltpu.make_async_copy(int_ref, tile_buf, local_sem.at[BATCH + 2])
+    for copy in (*locals_, cd_copy, ab_copy, int_copy):
+        copy.start()
+
+    barrier = pltpu.get_barrier_semaphore()
+    for dz in range(1, groups):
+        pl.semaphore_signal(barrier, inc=1, device_id=(t, lax.rem(g + dz, groups)), device_id_type=MESH)
+    for b in range(bits):
+        pl.semaphore_signal(barrier, inc=1, device_id=(flip(t, 1 << b), g), device_id_type=MESH)
+    pl.semaphore_wait(barrier, groups - 1 + bits)
+
+    events, sends = schedule(groups, tiles)
+    number = {node: i for i, node in enumerate(events)}
+    copies = {}
+
+    def forward(node):
+        half, k, m = node
+        block = buf.at[half, lax.rem(g - k + groups, groups), flip(t, m)]
+        for child, dim in sends[node]:
+            if dim == "z":
+                peer = (t, lax.rem(g + child[1], groups))
+            else:
+                peer = (flip(t, 1 << dim), g)
+            copy = pltpu.make_async_remote_copy(
+                src_ref=block, dst_ref=block, send_sem=send_sem.at[number[child]], recv_sem=recv_sem.at[number[child]],
+                device_id=peer, device_id_type=MESH)
+            copy.start()
+            copies[child] = copy
+
+    missing = {}
+    for half in range(BATCH):
+        for k in range(groups):
+            missing[half, k] = tiles
+    started = set()
+    scatters = []
+
+    def arrived(node):
+        half, k, _ = node
+        missing[half, k] -= 1
+        if missing[half, k]:
+            return
+        j = lax.rem(g - k + groups, groups)
+        cd = cd_smem[0, g * groups + j]
+        ab = ab_smem[0, g * groups + j]
+        operand = None
+        for c in range(buf.shape[-1] // widths):
+            chosen = jnp.full((1, 1, widths), (cd == c).astype(jnp.float32)).astype(buf.dtype)
+            part = buf[half, j, :, :, c * widths:(c + 1) * widths] * chosen
+            operand = part if operand is None else operand + part
+        product = jnp.dot(operand.reshape(-1, widths), tile_buf[0, j], preferred_element_type=jnp.float32)
+        for a in range(NT_DEV):
+            span = slice(a * widths, (a + 1) * widths)
+            term = product * (ab == a).astype(jnp.float32)
+            if half in started:
+                acc[half, :, span] += term
+            else:
+                acc[half, :, span] = term
+        started.add(half)
+        if all(missing[half, q] == 0 for q in range(groups)):
+            scatter(half)
+
+    def scatter(half):
+        for dz in range(1, groups):
+            peer = lax.rem(g + dz, groups)
+            piece = acc[half, pl.ds(pl.multiple_of(peer * rows, rows), rows), :]
+            send_buf[half, dz - 1] = piece.astype(send_buf.dtype)
+            slot = half * (groups - 1) + dz - 1
+            copy = pltpu.make_async_remote_copy(
+                src_ref=send_buf.at[half, dz - 1], dst_ref=sums_buf.at[half, dz - 1], send_sem=rs_send.at[slot],
+                recv_sem=rs_recv.at[slot], device_id=(t, peer), device_id_type=MESH)
+            copy.start()
+            scatters.append((half, copy))
+
+    for half in range(BATCH):
+        locals_[half].wait()
+        forward((half, 0, 0))
+    for copy in (cd_copy, ab_copy, int_copy):
+        copy.wait()
+    for half in range(BATCH):
+        arrived((half, 0, 0))
+    for node in events:
+        copies[node].wait_recv()
+        forward(node)
+        arrived(node)
+
+    for half in range(BATCH):
+        total = acc[half, pl.ds(pl.multiple_of(g * rows, rows), rows), :]
+        mine = [copy for owner, copy in scatters if owner == half]
+        for dz, copy in enumerate(mine):
+            copy.wait_recv()
+            total = total + sums_buf[half, dz].astype(jnp.float32)
+        out_ref[half] = (0.5 * total).astype(out_ref.dtype)
+    for node in events:
+        copies[node].wait_send()
+    for _, copy in scatters:
+        copy.wait_send()
+
+
+def fused(groups, tiles, amplitudes, integrals, slot_cd, slot_ab):
+    batch, pairs_dev, span = amplitudes.shape
+    widths = integrals.shape[-1]
+    pairs = pairs_dev * tiles
+    rows = pairs // groups
+    result = NT_DEV * widths
+    events, _ = schedule(groups, tiles)
+    count = len(events)
+    any_spec = pl.BlockSpec(memory_space=pl.ANY)
+    return pl.pallas_call(
+        functools.partial(kernel, groups, tiles),
+        out_shape=jax.ShapeDtypeStruct((batch, rows, result), jnp.bfloat16),
+        in_specs=[any_spec] * 4,
+        out_specs=pl.BlockSpec(memory_space=pltpu.VMEM),
+        scratch_shapes=[
+            pltpu.VMEM((batch, groups, tiles, pairs_dev, span), jnp.bfloat16),
+            pltpu.VMEM(integrals.shape, jnp.bfloat16),
+            pltpu.VMEM((batch, pairs, result), jnp.float32),
+            pltpu.VMEM((batch, groups - 1, rows, result), jnp.bfloat16),
+            pltpu.VMEM((batch, groups - 1, rows, result), jnp.bfloat16),
+            pltpu.SMEM(slot_cd.shape, jnp.int32),
+            pltpu.SMEM(slot_ab.shape, jnp.int32),
+            pltpu.SemaphoreType.DMA((batch + 3,)),
+            pltpu.SemaphoreType.DMA((count,)),
+            pltpu.SemaphoreType.DMA((count,)),
+            pltpu.SemaphoreType.DMA((batch * (groups - 1),)),
+            pltpu.SemaphoreType.DMA((batch * (groups - 1),)),
+        ],
+        compiler_params=pltpu.CompilerParams(collective_id=0, has_side_effects=True),
+    )(amplitudes, integrals, slot_cd, slot_ab)
 
 
 def accumulate(slot_operands, slot_tiles, ab_list):
@@ -18,7 +202,7 @@
     return summed.reshape(row_count, NT_DEV * widths)
 
 
-def per_device(amplitudes, integrals, slot_cd, slot_ab):
+def by_slabs(amplitudes, integrals, slot_cd, slot_ab):
     groups = lax.axis_size("grp")
     own_index = lax.axis_index("grp")
     widths = integrals.shape[-1]
@@ -41,6 +225,14 @@
 
 
 def solution(mesh):
+    groups, tiles = mesh.shape["grp"], mesh.shape["tile"]
+
+    def per_device(amplitudes, integrals, slot_cd, slot_ab):
+        gathered = amplitudes.size * amplitudes.dtype.itemsize * groups * tiles
+        if gathered > GATHER_LIMIT or tiles & (tiles - 1):
+            return by_slabs(amplitudes, integrals, slot_cd, slot_ab)
+        return fused(groups, tiles, amplitudes, integrals, slot_cd, slot_ab)
+
     return jax.shard_map(
         per_device,
         mesh=mesh,

time: 85.2 us -> 24.5 us (0.29)
  waiting for transfers between devices: 38.1 us -> 0 us
  Pallas kernels: 0 us -> 22.9 us
  blocking collectives: 18.4 us -> 0 us
  between operations: 13.5 us -> 0.01 us
  starting transfers between devices: 6.52 us -> 0 us
  other arithmetic: 3.5 us -> 0 us
  local copies, waits for them, and re-layouts: 3.82 us -> 1.38 us
  matrix products: 0.92 us -> 0 us
    reduce_scatter x2 -> x0, waiting for transfers between devices: 38 us -> none  [per_device(): lax.psum_scatter(full_terms, 'grp', scatter_dimension=0, tiled=True)]
    pallas_call x0 -> x1, Pallas kernels: none -> 22.9 us  [fused(): pl.pallas_call(functools.partial(kernel, groups, tiles), out_shape=jax.Sh...]
    all_gather x2 -> x0, blocking collectives: 18.4 us -> none  [per_device(): lax.all_gather(amplitudes[batch_index], 'tile', axis=0, tiled=True)]
    all_to_all x1 -> x0, starting transfers between devices: 6.48 us -> none  [per_device(): lax.all_to_all(own_tiles, 'grp', split_axis=0, concat_axis=0, tiled=True)]
    another operation x3 -> x0, other arithmetic: 2.14 us -> none  [per_device(): return jnp.stack(outputs)]
    unnamed x2 -> x0, other arithmetic: 1.34 us -> none
    gather x2 -> x0, local copies, waits for them, and re-layouts: 1.11 us -> none  [per_device(): operands = jnp.take(blocks, cd_list, axis=1)]
    dot_general x4 -> x0, matrix products: 0.92 us -> none  [the longest x2 0.5 us: accumulate(): jnp.einsum('rsc,scd->rsd', slot_operands, slot_tiles, preferred_element_t...]
  transfers between devices with their start and end apart: 3 -> 0, of which waited for: 2 -> 0; matrix products, arithmetic and copies ran while one was open for 7% -> 0% of each run, Pallas kernels for 0% -> 0%
where the time goes in v1:
time: 24.5 us; the launch traced here: 24.3 us
  Pallas kernels  22.9 us (93%)
  local copies, waits for them, and re-layouts  1.38 us (6%)
    pallas_call x1, Pallas kernels, fused(): pl.pallas_call(functools.partial(kernel, groups, tiles), out_shape=jax.Sh...  22.9 us
    unnamed x1, local copies, waits for them, and re-layouts  1.38 us

profile of v1, /device:TPU:0, one launch (start us, length us, event | category | flops | bytes accessed | tf_op | source)
XLA Modules:
  0.0 24.3 jit_solution(11362183114967082405)
XLA Ops:
  0.0 22.9 %shard_map.46 = bf16[2,16,512]{2,1,0:T(8,128)(2,1)} custom-call(bf16[2,8,1024]{2,1,0:T(8,128)(2,1)} %amp_ref.1, bf16[1,4,256,256]{3,2,1,0:T(8,128)(2,1)} %int_ref.1, s32[1,16]{1,0:T(1,128)} %cd_ref.1, s32[1,16]{1,0:T(1,128)} %ab_ref.1), custom_call_target="tpu_custom_call" | custom-call | tf_op jit(solution)/shard_map/pallas_call | solution.py:171
  23.0 1.4 %copy.6 = bf16[2,16,512]{2,1,0:T(8,128)(2,1)} copy(bf16[2,16,512]{2,1,0:T(8,128)(2,1)} %shard_map.46) | data formatting | bytes 65536

commit v2 on v0

--- a/solution.py
+++ b/solution.py
@@ -1,10 +1,161 @@
+import functools
+
 import jax
 import jax.numpy as jnp
 from jax import lax
+from jax.experimental import pallas as pl
+from jax.experimental.pallas import tpu as pltpu
 from jax.sharding import PartitionSpec as P
 
+MESH = pl.DeviceIdType.MESH
 NT_DEV = 2
 BATCH = 2
+GATHER_LIMIT = 8 * 2**20
+CORES = 2
+
+
+def kernel(groups, places, amp_ref, int_ref, cd_ref, ab_ref, out_ref, buf, tile_buf, acc, send_buf, sums_buf,
+           cd_smem, ab_smem, local_sem, z_send, z_recv, p_send, p_recv, c_send, c_recv, rs_send, rs_recv):
+    g, t = lax.axis_index("grp"), lax.axis_index("tile")
+    place, core = lax.div(t, jnp.int32(CORES)), lax.rem(t, jnp.int32(CORES))
+    widths = int_ref.shape[-1]
+    pairs_dev = amp_ref.shape[1]
+    share = places // groups
+    group = [lax.rem(g + k, groups) for k in range(groups)]
+    source = [lax.rem(g - k + groups, groups) for k in range(groups)]
+    spot = [lax.rem(place + q, places) for q in range(places)]
+    origin = [lax.rem(place - q + places, places) for q in range(places)]
+    cores = (core, 1 - core)
+
+    amp_copy = pltpu.make_async_copy(amp_ref, buf.at[g, core, place], local_sem.at[0])
+    cd_copy = pltpu.make_async_copy(cd_ref, cd_smem, local_sem.at[1])
+    ab_copy = pltpu.make_async_copy(ab_ref, ab_smem, local_sem.at[2])
+    int_copy = pltpu.make_async_copy(int_ref, tile_buf, local_sem.at[3])
+    for copy in (amp_copy, cd_copy, ab_copy, int_copy):
+        copy.start()
+
+    barrier = pltpu.get_barrier_semaphore()
+    peers = [(t, group[k]) for k in range(1, groups)]
+    peers += [(spot[q] * CORES + core, g) for q in range(1, places)]
+    peers += [(place * CORES + 1 - core, g)]
+    for peer in peers:
+        pl.semaphore_signal(barrier, inc=1, device_id=peer, device_id_type=MESH)
+    pl.semaphore_wait(barrier, len(peers))
+
+    def remote(src, dst, send, recv, peer):
+        copy = pltpu.make_async_remote_copy(
+            src_ref=src, dst_ref=dst, send_sem=send, recv_sem=recv, device_id=peer, device_id_type=MESH)
+        copy.start()
+        return copy
+
+    def spread(k):
+        block = buf.at[source[k], core, place]
+        return [
+            remote(block, block, p_send.at[k, q - 1], p_recv.at[k, q - 1], (spot[q] * CORES + core, g))
+            for q in range(1, places)
+        ]
+
+    def multiply(k, part):
+        j = source[k]
+        cd = cd_smem[0, g * groups + j]
+        ab = ab_smem[0, g * groups + j]
+        operand = None
+        for c in range(buf.shape[-1] // widths):
+            chosen = jnp.full((1, 1, 1, widths), (cd == c).astype(jnp.float32)).astype(buf.dtype)
+            block = buf[j, cores[part], :, :, :, c * widths:(c + 1) * widths] * chosen
+            operand = block if operand is None else operand + block
+        product = jnp.dot(operand.reshape(-1, widths), tile_buf[0, j], preferred_element_type=jnp.float32)
+        product = product.reshape(*operand.shape[:3], widths)
+        for a in range(NT_DEV):
+            span = slice(a * widths, (a + 1) * widths)
+            term = product * (ab == a).astype(jnp.float32)
+            if k:
+                acc[part, :, :, :, span] += term
+            else:
+                acc[part, :, :, :, span] = term
+
+    def scatter(part):
+        out = []
+        for k in range(1, groups):
+            piece = acc[part, pl.ds(group[k] * share, share)]
+            send_buf[part, k - 1] = piece.astype(send_buf.dtype)
+            out.append(remote(send_buf.at[part, k - 1], sums_buf.at[part, k - 1], rs_send.at[part, k - 1],
+                              rs_recv.at[part, k - 1], (t, group[k])))
+        return out
+
+    amp_copy.wait()
+    own = buf.at[g, core, place]
+    along = [remote(own, own, z_send.at[k - 1], z_recv.at[k - 1], (t, group[k])) for k in range(1, groups)]
+    spreads = [spread(0)]
+    for k in range(1, groups):
+        along[k - 1].wait_recv()
+        spreads.append(spread(k))
+    for copy in (cd_copy, ab_copy, int_copy):
+        copy.wait()
+    crossings = []
+    scatters = []
+    for k in range(groups):
+        for copy in spreads[k]:
+            copy.wait_recv()
+        half = buf.at[source[k], core]
+        crossings.append(remote(half, half, c_send.at[k], c_recv.at[k], (place * CORES + 1 - core, g)))
+        multiply(k, 0)
+        if k == groups - 1:
+            scatters.append(scatter(0))
+        if k:
+            crossings[k - 1].wait_recv()
+            multiply(k - 1, 1)
+    crossings[-1].wait_recv()
+    multiply(groups - 1, 1)
+    scatters.append(scatter(1))
+
+    for part in range(CORES):
+        total = acc[part, pl.ds(g * share, share)]
+        for k in range(1, groups):
+            scatters[part][k - 1].wait_recv()
+            total = total + sums_buf[part, k - 1].astype(jnp.float32)
+        total = (0.5 * total).astype(out_ref.dtype)
+        for at in range(share):
+            first = pl.multiple_of((at * CORES + cores[part]) * pairs_dev, pairs_dev)
+            out_ref[:, pl.ds(first, pairs_dev), :] = total[at]
+    for copy in (*along, *crossings, *(c for group_ in spreads + scatters for c in group_)):
+        copy.wait_send()
+
+
+def fused(groups, tiles, amplitudes, integrals, slot_cd, slot_ab):
+    batch, pairs_dev, span = amplitudes.shape
+    widths = integrals.shape[-1]
+    places = tiles // CORES
+    rows = pairs_dev * tiles // groups
+    result = NT_DEV * widths
+    any_spec = pl.BlockSpec(memory_space=pl.ANY)
+    piece = (CORES, groups - 1, places // groups, batch, pairs_dev, result)
+    dma = pltpu.SemaphoreType.DMA
+    return pl.pallas_call(
+        functools.partial(kernel, groups, places),
+        out_shape=jax.ShapeDtypeStruct((batch, rows, result), jnp.bfloat16),
+        in_specs=[any_spec] * 4,
+        out_specs=pl.BlockSpec(memory_space=pltpu.VMEM),
+        scratch_shapes=[
+            pltpu.VMEM((groups, CORES, places, batch, pairs_dev, span), jnp.bfloat16),
+            pltpu.VMEM(integrals.shape, jnp.bfloat16),
+            pltpu.VMEM((CORES, places, batch, pairs_dev, result), jnp.float32),
+            pltpu.VMEM(piece, jnp.bfloat16),
+            pltpu.VMEM(piece, jnp.bfloat16),
+            pltpu.SMEM(slot_cd.shape, jnp.int32),
+            pltpu.SMEM(slot_ab.shape, jnp.int32),
+            dma((4,)),
+            dma((groups - 1,)),
+            dma((groups - 1,)),
+            dma((groups, places - 1)),
+            dma((groups, places - 1)),
+            dma((groups,)),
+            dma((groups,)),
+            dma((CORES, groups - 1)),
+            dma((CORES, groups - 1)),
+        ],
+        compiler_params=pltpu.CompilerParams(collective_id=0, has_side_effects=True),
+    )(amplitudes, integrals, slot_cd, slot_ab)
 
 
 def accumulate(slot_operands, slot_tiles, ab_list):
@@ -18,7 +169,7 @@
     return summed.reshape(row_count, NT_DEV * widths)
 
 
-def per_device(amplitudes, integrals, slot_cd, slot_ab):
+def by_slabs(amplitudes, integrals, slot_cd, slot_ab):
     groups = lax.axis_size("grp")
     own_index = lax.axis_index("grp")
     widths = integrals.shape[-1]
@@ -41,6 +192,14 @@
 
 
 def solution(mesh):
+    groups, tiles = mesh.shape["grp"], mesh.shape["tile"]
+
+    def per_device(amplitudes, integrals, slot_cd, slot_ab):
+        gathered = amplitudes.size * amplitudes.dtype.itemsize * groups * tiles
+        if gathered > GATHER_LIMIT or tiles % (CORES * groups):
+            return by_slabs(amplitudes, integrals, slot_cd, slot_ab)
+        return fused(groups, tiles, amplitudes, integrals, slot_cd, slot_ab)
+
     return jax.shard_map(
         per_device,
         mesh=mesh,

time: 85.2 us -> 22.2 us (0.26)
  waiting for transfers between devices: 38.1 us -> 0 us
  Pallas kernels: 0 us -> 20.6 us
  blocking collectives: 18.4 us -> 0 us
  between operations: 13.5 us -> 0.01 us
  starting transfers between devices: 6.52 us -> 0 us
  other arithmetic: 3.5 us -> 0 us
  local copies, waits for them, and re-layouts: 3.82 us -> 1.38 us
  matrix products: 0.92 us -> 0 us
    reduce_scatter x2 -> x0, waiting for transfers between devices: 38 us -> none  [per_device(): lax.psum_scatter(full_terms, 'grp', scatter_dimension=0, tiled=True)]
    pallas_call x0 -> x1, Pallas kernels: none -> 20.6 us  [fused(): pl.pallas_call(functools.partial(kernel, groups, places), out_shape=jax.S...]
    all_gather x2 -> x0, blocking collectives: 18.4 us -> none  [per_device(): lax.all_gather(amplitudes[batch_index], 'tile', axis=0, tiled=True)]
    all_to_all x1 -> x0, starting transfers between devices: 6.48 us -> none  [per_device(): lax.all_to_all(own_tiles, 'grp', split_axis=0, concat_axis=0, tiled=True)]
    another operation x3 -> x0, other arithmetic: 2.14 us -> none  [per_device(): return jnp.stack(outputs)]
    unnamed x2 -> x0, other arithmetic: 1.34 us -> none
    gather x2 -> x0, local copies, waits for them, and re-layouts: 1.11 us -> none  [per_device(): operands = jnp.take(blocks, cd_list, axis=1)]
    dot_general x4 -> x0, matrix products: 0.92 us -> none  [the longest x2 0.5 us: accumulate(): jnp.einsum('rsc,scd->rsd', slot_operands, slot_tiles, preferred_element_t...]
  transfers between devices with their start and end apart: 3 -> 0, of which waited for: 2 -> 0; matrix products, arithmetic and copies ran while one was open for 7% -> 0% of each run, Pallas kernels for 0% -> 0%
where the time goes in v2:
time: 22.2 us; the launch traced here: 22 us
  Pallas kernels  20.6 us (93%)
  local copies, waits for them, and re-layouts  1.38 us (6%)
    pallas_call x1, Pallas kernels, fused(): pl.pallas_call(functools.partial(kernel, groups, places), out_shape=jax.S...  20.6 us
    unnamed x1, local copies, waits for them, and re-layouts  1.38 us

profile of v2, /device:TPU:0, one launch (start us, length us, event | category | flops | bytes accessed | tf_op | source)
XLA Modules:
  0.0 22.0 jit_solution(3165157491864364057)
XLA Ops:
  0.0 20.6 %shard_map.46 = bf16[2,16,512]{2,1,0:T(8,128)(2,1)} custom-call(bf16[2,8,1024]{2,1,0:T(8,128)(2,1)} %amp_ref.1, bf16[1,4,256,256]{3,2,1,0:T(8,128)(2,1)} %int_ref.1, s32[1,16]{1,0:T(1,128)} %cd_ref.1, s32[1,16]{1,0:T(1,128)} %ab_ref.1), custom_call_target="tpu_custom_call" | custom-call | tf_op jit(solution)/shard_map/pallas_call | solution.py:134
  20.6 1.4 %copy.6 = bf16[2,16,512]{2,1,0:T(8,128)(2,1)} copy(bf16[2,16,512]{2,1,0:T(8,128)(2,1)} %shard_map.46) | data formatting | bytes 65536
